TPU v7x, 32 devices: a whole 2x2x4 slice. The times are simulated.
32 devices in a mesh: dp: 8 (over y, x, core), seq: 4 (over z).
Axes of the slice: x: 2, y: 2, z: 4, core: 2. Of those that a mesh axis runs over, the one named last changes fastest.
Arguments:
- encoder_input: bfloat16 [8, 1024, 512], P('dp', 'seq'), may hold values from -75 to 75, as said below
- decoder_input: bfloat16 [8, 1024, 512], P('dp', 'seq'), may hold values from -75 to 75, as said below
- output_grad: bfloat16 [8, 1024, 512], P('dp', 'seq'), may hold values from -6 to 6
- segment_lengths: int32 [8, 4], P('dp'), may hold values from 1 to 772, as said below
- bucket_table: int32 [2047], replicated, may hold values from 0 to 31, as said below
- enc_gain1: float32 [512], replicated, may hold values from 0.25 to 1.75
- enc_qkv: bfloat16 [512, 1536], replicated, may hold values from -0.125 to 0.125
- enc_proj: bfloat16 [512, 512], replicated, may hold values from -1.5 to 1.5
- enc_rel: float32 [32, 8], replicated, may hold values from -4 to 4
- enc_gain2: float32 [512], replicated, may hold values from 0.25 to 1.75
- enc_wi: bfloat16 [512, 2048], replicated, may hold values from -0.25 to 0.25
- enc_wo: bfloat16 [2048, 512], replicated, may hold values from -0.1875 to 0.1875
- enc_gainf: float32 [512], replicated, may hold values from 0.25 to 1.75
- dec_gain1: float32 [512], replicated, may hold values from 0.25 to 1.75
- dec_qkv: bfloat16 [512, 1536], replicated, may hold values from -0.125 to 0.125
- dec_proj: bfloat16 [512, 512], replicated, may hold values from -1.5 to 1.5
- dec_rel: float32 [32, 8], replicated, may hold values from -4 to 4
- dec_gain2: float32 [512], replicated, may hold values from 0.25 to 1.75
- cross_q: bfloat16 [512, 512], replicated, may hold values from -0.125 to 0.125
- cross_kv: bfloat16 [512, 1024], replicated, may hold values from -0.125 to 0.125
- cross_proj: bfloat16 [512, 512], replicated, may hold values from -1.5 to 1.5
- dec_gain3: float32 [512], replicated, may hold values from 0.25 to 1.75
- dec_wi: bfloat16 [512, 2048], replicated, may hold values from -0.25 to 0.25
- dec_wo: bfloat16 [2048, 512], replicated, may hold values from -0.1875 to 0.1875
Outputs:
- dec_output: bfloat16 [8, 1024, 512], P('dp', 'seq')
- encoder_grad: bfloat16 [8, 1024, 512], P('dp', 'seq')
- decoder_grad: bfloat16 [8, 1024, 512], P('dp', 'seq')
- sublayer_rms: float32 [8], replicated
- enc_gain1_grad: float32 [512], replicated
- enc_qkv_grad: float32 [512, 1536], P('dp', 'seq')
- enc_proj_grad: float32 [512, 512], P('dp', 'seq')
- enc_rel_grad: float32 [32, 8], replicated
- enc_gain2_grad: float32 [512], replicated
- enc_wi_grad: float32 [512, 2048], P('dp', 'seq')
- enc_wo_grad: float32 [2048, 512], P('dp', 'seq')
- enc_gainf_grad: float32 [512], replicated
- dec_gain1_grad: float32 [512], replicated
- dec_qkv_grad: float32 [512, 1536], P('dp', 'seq')
- dec_proj_grad: float32 [512, 512], P('dp', 'seq')
- dec_rel_grad: float32 [32, 8], replicated
- dec_gain2_grad: float32 [512], replicated
- cross_q_grad: float32 [512, 512], P('dp', 'seq')
- cross_kv_grad: float32 [512, 1024], P('dp', 'seq')
- cross_proj_grad: float32 [512, 512], P('dp', 'seq')
- dec_gain3_grad: float32 [512], replicated
- dec_wi_grad: float32 [512, 2048], P('dp', 'seq')
- dec_wo_grad: float32 [2048, 512], P('dp', 'seq')
Inputs may be any that keep to these rules, and one draw needn't show every extreme that they name: `segment_lengths`: each row's 4 lengths add up to 1024; one of them, at a place drawn for the row, is the largest; the others are 1 or more, and in every row one of them is 1. `bucket_table`: offset 0 is bucket 0; negative offsets use the first 16 buckets and positive ones the rest; within each direction the bucket never falls as the distance grows. `encoder_input`: Real-valued activations. `decoder_input`: Real-valued activations.
All inputs are finite; a program needn't handle non-finite values.
Results may differ from a plain program's by a relative error of at most 0.025.
Values may be sent and summed in bfloat16 or wider, within the bound.
No kernel may reach another device: no remote copies, remote signals or barrier semaphores. Data moves between devices by JAX's collectives and lax.ppermute only.
A program may use at most 192 MiB of HBM per device.

v0:
```python
from functools import partial

import jax
import jax.numpy as jnp
from jax import lax
from jax.sharding import PartitionSpec as P

HEAD_DIM = 64


eps_norm = 1e-06
negative = -1000000000.0


def rms_norm(values, gain_vec):
    return (
        values * lax.rsqrt(jnp.mean(values * values, axis=-1, keepdims=True) + eps_norm) * gain_vec
    )


def norm_back(values, gain_vec, incoming):
    _, pull = jax.vjp(rms_norm, values, gain_vec)
    return pull(incoming)


def gelu_back(hidden, incoming):
    _, pull = jax.vjp(partial(jax.nn.gelu, approximate=True), hidden)
    return pull(incoming)[0]


def dense(acts, weight):
    return jnp.einsum("rqi,io->rqo", acts, weight, preferred_element_type=jnp.float32)


def dense_back(incoming, weight):
    return jnp.einsum("rqo,io->rqi", incoming, weight, preferred_element_type=jnp.float32)


def weight_grad(acts, incoming):
    return jnp.einsum("rqi,rqo->io", acts, incoming, preferred_element_type=jnp.float32)


def split_heads(tensor):
    return tensor.reshape(tensor.shape[0], tensor.shape[1], -1, HEAD_DIM)


def segment_ids(lengths_arr, length):
    seg_ends = jnp.cumsum(lengths_arr, axis=1)
    places = jnp.arange(length, dtype=jnp.int32)
    return jnp.sum((places[None, :, None] >= seg_ends[:, None, :]).astype(jnp.int32), axis=2)


def bucket_onehot(lookup, first_pos, row_count, length, bucket_count):
    width_all = length + row_count - 1
    window = lax.dynamic_slice_in_dim(lookup, length - first_pos - row_count, width_all)
    return (window[:, None] == jnp.arange(bucket_count, dtype=jnp.int32)[None, :]).astype(
        jnp.float32
    )


def position_bias(rel_table, lookup, first_pos, row_count, length):
    onehot = bucket_onehot(lookup, first_pos, row_count, length, rel_table.shape[0])
    width_all = length + row_count - 1
    per_offset = jnp.dot(onehot, rel_table, precision=lax.Precision.HIGHEST).T
    padded = jnp.pad(per_offset, ((0, 0), (0, 1)))
    repeated = jnp.tile(padded, (1, row_count))
    trimmed = repeated[:, row_count - 1 : row_count - 1 + row_count * width_all]
    return trimmed.reshape(-1, row_count, width_all)[:, :, :length]


def bias_grad(grad_sum, lookup, first_pos, bucket_count):
    head_count, row_count, length = grad_sum.shape
    width_all = length + row_count - 1
    padded = jnp.pad(grad_sum, ((0, 0), (0, 0), (0, row_count)))
    flat_grad = jnp.pad(padded.reshape(head_count, -1), ((0, 0), (row_count - 1, 1)))
    skewed = flat_grad.reshape(head_count, row_count, length + row_count + 1)[:, :, :width_all]
    per_offset = jnp.sum(skewed, axis=1)
    onehot = bucket_onehot(lookup, first_pos, row_count, length, bucket_count)
    return jnp.dot(onehot.T, per_offset.T, precision=lax.Precision.HIGHEST)


def raw_scores(queries, key_rows, pos_bias, allowed):
    scores = jnp.einsum(
        "rqhd,rkhd->rhqk",
        split_heads(queries),
        split_heads(key_rows),
        preferred_element_type=jnp.float32,
    )
    if pos_bias is not None:
        scores = scores + pos_bias[None]
    return jnp.where(allowed[:, None], scores, negative)


def attend_fwd(queries, key_rows, values, pos_bias, allowed):
    scores = raw_scores(queries, key_rows, pos_bias, allowed)
    row_max = jnp.max(scores, axis=-1, keepdims=True)
    exponent = jnp.exp(scores - row_max)
    row_sum = jnp.sum(exponent, axis=-1, keepdims=True)
    probs_low = (exponent / row_sum).astype(jnp.bfloat16)
    mixed = jnp.einsum(
        "rhqk,rkhd->rqhd", probs_low, split_heads(values), preferred_element_type=jnp.float32
    )
    return (mixed.reshape(queries.shape), row_max + jnp.log(row_sum))


def attend_back(queries, key_rows, values, pos_bias, allowed, log_total, incoming):
    scores = raw_scores(queries, key_rows, pos_bias, allowed)
    probs_f = jnp.exp(scores - log_total)
    grad_heads = split_heads(incoming)
    grad_values = jnp.einsum(
        "rhqk,rqhd->rkhd",
        probs_f.astype(jnp.bfloat16),
        grad_heads,
        preferred_element_type=jnp.float32,
    )
    grad_probs = jnp.einsum(
        "rqhd,rkhd->rhqk", grad_heads, split_heads(values), preferred_element_type=jnp.float32
    )
    grad_scores = (
        probs_f * (grad_probs - jnp.sum(probs_f * grad_probs, axis=-1, keepdims=True))
    ).astype(jnp.bfloat16)
    grad_queries = jnp.einsum(
        "rhqk,rkhd->rqhd", grad_scores, split_heads(key_rows), preferred_element_type=jnp.float32
    )
    grad_keys = jnp.einsum(
        "rhqk,rqhd->rkhd", grad_scores, split_heads(queries), preferred_element_type=jnp.float32
    )
    bias_sum = jnp.sum(grad_scores, axis=0, dtype=jnp.float32)
    return (
        grad_queries.reshape(queries.shape),
        grad_keys.reshape(key_rows.shape),
        grad_values.reshape(key_rows.shape),
        bias_sum,
    )


def flatten_all(members):
    return jnp.concatenate([member.reshape(-1) for member in members])


def unflatten(flat_grad, members):
    result = []
    offset = 0
    for member in members:
        result.append(flat_grad[offset : offset + member.size].reshape(member.shape))
        offset += member.size
    return result


def on_device(
    encoder_input,
    decoder_input,
    output_grad,
    segment_lengths,
    bucket_table,
    enc_gain1,
    enc_qkv,
    enc_proj,
    enc_rel,
    enc_gain2,
    enc_wi,
    enc_wo,
    enc_gainf,
    dec_gain1,
    dec_qkv,
    dec_proj,
    dec_rel,
    dec_gain2,
    cross_q,
    cross_kv,
    cross_proj,
    dec_gain3,
    dec_wi,
    dec_wo,
):
    bf_type = jnp.bfloat16
    seq_count = lax.axis_size("seq")
    device_count = lax.axis_size(("dp", "seq"))
    row_count, query_len, model_width = encoder_input.shape
    full_len = query_len * seq_count
    first_pos = lax.axis_index("seq") * query_len
    inner_width = enc_proj.shape[0]
    bucket_count = enc_rel.shape[0]
    ids_full = segment_ids(segment_lengths, full_len)
    ids_own = lax.dynamic_slice_in_dim(ids_full, first_pos, query_len, axis=1)
    same_seg = ids_own[:, :, None] == ids_full[:, None, :]
    key_pos = jnp.arange(full_len, dtype=jnp.int32)
    query_pos = first_pos + jnp.arange(query_len, dtype=jnp.int32)
    causal = same_seg & (key_pos[None, None, :] <= query_pos[None, :, None])
    enc_bias = position_bias(enc_rel, bucket_table, first_pos, query_len, full_len)
    dec_bias = position_bias(dec_rel, bucket_table, first_pos, query_len, full_len)
    enc_in = encoder_input.astype(jnp.float32)
    enc_a = rms_norm(enc_in, enc_gain1).astype(bf_type)
    enc_three = dense(enc_a, enc_qkv).astype(bf_type)
    enc_query = enc_three[..., :inner_width]
    enc_keys_all, enc_vals_all = (
        lax.all_gather(enc_three[..., inner_width : 2 * inner_width], "seq", axis=1, tiled=True),
        lax.all_gather(enc_three[..., 2 * inner_width :], "seq", axis=1, tiled=True),
    )
    enc_mix, enc_lse = attend_fwd(enc_query, enc_keys_all, enc_vals_all, enc_bias, same_seg)
    enc_mix_low = enc_mix.astype(bf_type)
    enc_att = dense(enc_mix_low, enc_proj)
    enc_h1 = enc_in + enc_att
    enc_b = rms_norm(enc_h1, enc_gain2).astype(bf_type)
    enc_u = dense(enc_b, enc_wi)
    enc_g = jax.nn.gelu(enc_u, approximate=True).astype(bf_type)
    enc_ffn = dense(enc_g, enc_wo)
    enc_h2 = enc_h1 + enc_ffn
    encoded = rms_norm(enc_h2, enc_gainf).astype(bf_type)
    dec_in = decoder_input.astype(jnp.float32)
    dec_a = rms_norm(dec_in, dec_gain1).astype(bf_type)
    dec_three = dense(dec_a, dec_qkv).astype(bf_type)
    dec_query = dec_three[..., :inner_width]
    dec_keys_all, dec_vals_all = (
        lax.all_gather(dec_three[..., inner_width : 2 * inner_width], "seq", axis=1, tiled=True),
        lax.all_gather(dec_three[..., 2 * inner_width :], "seq", axis=1, tiled=True),
    )
    dec_mix, dec_lse = attend_fwd(dec_query, dec_keys_all, dec_vals_all, dec_bias, causal)
    dec_mix_low = dec_mix.astype(bf_type)
    dec_att = dense(dec_mix_low, dec_proj)
    dec_h1 = dec_in + dec_att
    dec_c = rms_norm(dec_h1, dec_gain2).astype(bf_type)
    cross_query = dense(dec_c, cross_q).astype(bf_type)
    cross_pair = dense(encoded, cross_kv).astype(bf_type)
    cross_keys_all, cross_vals_all = (
        lax.all_gather(cross_pair[..., :inner_width], "seq", axis=1, tiled=True),
        lax.all_gather(cross_pair[..., inner_width:], "seq", axis=1, tiled=True),
    )
    cross_mix, cross_lse = attend_fwd(cross_query, cross_keys_all, cross_vals_all, None, same_seg)
    cross_mix_low = cross_mix.astype(bf_type)
    cross_att = dense(cross_mix_low, cross_proj)
    dec_h2 = dec_h1 + cross_att
    dec_b = rms_norm(dec_h2, dec_gain3).astype(bf_type)
    dec_u = dense(dec_b, dec_wi)
    dec_g = jax.nn.gelu(dec_u, approximate=True).astype(bf_type)
    dec_ffn = dense(dec_g, dec_wo)
    dec_h3 = dec_h2 + dec_ffn
    dec_output = dec_h3.astype(bf_type)
    stat_terms = jnp.stack(
        [
            jnp.sum(member * member)
            for member in (enc_att, enc_h1, enc_ffn, enc_h2, dec_att, cross_att, dec_ffn, dec_h3)
        ]
    )
    stat_total = lax.psum(stat_terms, ("dp", "seq"))
    stat_members = []
    top_grad = output_grad.astype(jnp.float32)
    dec_ffn_grad = top_grad.astype(bf_type)
    dec_wo_grad = weight_grad(dec_g, dec_ffn_grad)
    dec_u_grad = gelu_back(dec_u, dense_back(dec_ffn_grad, dec_wo)).astype(bf_type)
    dec_wi_grad = weight_grad(dec_b, dec_u_grad)
    dec_h2_part, dec_gain3_grad = norm_back(dec_h2, dec_gain3, dense_back(dec_u_grad, dec_wi))
    dec_h2_grad = top_grad + dec_h2_part
    cross_att_grad = dec_h2_grad.astype(bf_type)
    cross_proj_grad = weight_grad(cross_mix_low, cross_att_grad)
    cross_mix_grad = dense_back(cross_att_grad, cross_proj).astype(bf_type)
    cross_q_part, cross_k_part, cross_v_part, _ = attend_back(
        cross_query, cross_keys_all, cross_vals_all, None, same_seg, cross_lse, cross_mix_grad
    )
    cross_k_grad, cross_v_grad = (
        lax.psum_scatter(
            cross_k_part.astype(jnp.bfloat16), "seq", scatter_dimension=1, tiled=True
        ).astype(jnp.float32),
        lax.psum_scatter(
            cross_v_part.astype(jnp.bfloat16), "seq", scatter_dimension=1, tiled=True
        ).astype(jnp.float32),
    )
    cross_pair_grad = jnp.concatenate([cross_k_grad, cross_v_grad], axis=-1).astype(bf_type)
    cross_query_grad = cross_q_part.astype(bf_type)
    cross_q_grad = weight_grad(dec_c, cross_query_grad)
    cross_kv_grad = weight_grad(encoded, cross_pair_grad)
    encoded_grad = dense_back(cross_pair_grad, cross_kv)
    dec_h1_part, dec_gain2_grad = norm_back(
        dec_h1, dec_gain2, dense_back(cross_query_grad, cross_q)
    )
    dec_h1_grad = dec_h2_grad + dec_h1_part
    dec_att_grad = dec_h1_grad.astype(bf_type)
    dec_proj_grad = weight_grad(dec_mix_low, dec_att_grad)
    dec_mix_grad = dense_back(dec_att_grad, dec_proj).astype(bf_type)
    dec_q_part, dec_k_part, dec_v_part, dec_bias_sum = attend_back(
        dec_query, dec_keys_all, dec_vals_all, dec_bias, causal, dec_lse, dec_mix_grad
    )
    dec_k_grad, dec_v_grad = (
        lax.psum_scatter(
            dec_k_part.astype(jnp.bfloat16), "seq", scatter_dimension=1, tiled=True
        ).astype(jnp.float32),
        lax.psum_scatter(
            dec_v_part.astype(jnp.bfloat16), "seq", scatter_dimension=1, tiled=True
        ).astype(jnp.float32),
    )
    dec_three_grad = jnp.concatenate([dec_q_part, dec_k_grad, dec_v_grad], axis=-1).astype(bf_type)
    dec_qkv_grad = weight_grad(dec_a, dec_three_grad)
    dec_in_part, dec_gain1_grad = norm_back(dec_in, dec_gain1, dense_back(dec_three_grad, dec_qkv))
    decoder_grad = (dec_h1_grad + dec_in_part).astype(bf_type)
    dec_rel_grad = bias_grad(dec_bias_sum, bucket_table, first_pos, bucket_count)
    enc_h2_grad, enc_gainf_grad = norm_back(enc_h2, enc_gainf, encoded_grad)
    enc_ffn_grad = enc_h2_grad.astype(bf_type)
    enc_wo_grad = weight_grad(enc_g, enc_ffn_grad)
    enc_u_grad = gelu_back(enc_u, dense_back(enc_ffn_grad, enc_wo)).astype(bf_type)
    enc_wi_grad = weight_grad(enc_b, enc_u_grad)
    enc_h1_part, enc_gain2_grad = norm_back(enc_h1, enc_gain2, dense_back(enc_u_grad, enc_wi))
    enc_h1_grad = enc_h2_grad + enc_h1_part
    enc_att_grad = enc_h1_grad.astype(bf_type)
    enc_proj_grad = weight_grad(enc_mix_low, enc_att_grad)
    enc_mix_grad = dense_back(enc_att_grad, enc_proj).astype(bf_type)
    enc_q_part, enc_k_part, enc_v_part, enc_bias_sum = attend_back(
        enc_query, enc_keys_all, enc_vals_all, enc_bias, same_seg, enc_lse, enc_mix_grad
    )
    enc_k_grad, enc_v_grad = (
        lax.psum_scatter(
            enc_k_part.astype(jnp.bfloat16), "seq", scatter_dimension=1, tiled=True
        ).astype(jnp.float32),
        lax.psum_scatter(
            enc_v_part.astype(jnp.bfloat16), "seq", scatter_dimension=1, tiled=True
        ).astype(jnp.float32),
    )
    enc_three_grad = jnp.concatenate([enc_q_part, enc_k_grad, enc_v_grad], axis=-1).astype(bf_type)
    enc_qkv_grad = weight_grad(enc_a, enc_three_grad)
    enc_in_part, enc_gain1_grad = norm_back(enc_in, enc_gain1, dense_back(enc_three_grad, enc_qkv))
    encoder_grad = (enc_h1_grad + enc_in_part).astype(bf_type)
    enc_rel_grad = bias_grad(enc_bias_sum, bucket_table, first_pos, bucket_count)
    small_members = stat_members + [
        enc_gain1_grad,
        enc_rel_grad,
        enc_gain2_grad,
        enc_gainf_grad,
        dec_gain1_grad,
        dec_rel_grad,
        dec_gain2_grad,
        dec_gain3_grad,
    ]
    small_total = unflatten(lax.psum(flatten_all(small_members), ("dp", "seq")), small_members)
    (
        enc_gain1_sum,
        enc_rel_sum,
        enc_gain2_sum,
        enc_gainf_sum,
        dec_gain1_sum,
        dec_rel_sum,
        dec_gain2_sum,
        dec_gain3_sum,
    ) = small_total
    partial_rows = (
        lax.psum_scatter(enc_qkv_grad, "dp", scatter_dimension=0, tiled=True),
        lax.psum_scatter(enc_proj_grad, "dp", scatter_dimension=0, tiled=True),
        lax.psum_scatter(enc_wi_grad, "dp", scatter_dimension=0, tiled=True),
        lax.psum_scatter(enc_wo_grad, "dp", scatter_dimension=0, tiled=True),
        lax.psum_scatter(dec_qkv_grad, "dp", scatter_dimension=0, tiled=True),
        lax.psum_scatter(dec_proj_grad, "dp", scatter_dimension=0, tiled=True),
        lax.psum_scatter(cross_q_grad, "dp", scatter_dimension=0, tiled=True),
        lax.psum_scatter(cross_kv_grad, "dp", scatter_dimension=0, tiled=True),
        lax.psum_scatter(cross_proj_grad, "dp", scatter_dimension=0, tiled=True),
        lax.psum_scatter(dec_wi_grad, "dp", scatter_dimension=0, tiled=True),
        lax.psum_scatter(dec_wo_grad, "dp", scatter_dimension=0, tiled=True),
    )
    blocks = (
        lax.psum_scatter(
            partial_rows[0].astype(jnp.bfloat16), "seq", scatter_dimension=1, tiled=True
        ).astype(jnp.float32),
        lax.psum_scatter(
            partial_rows[1].astype(jnp.bfloat16), "seq", scatter_dimension=1, tiled=True
        ).astype(jnp.float32),
        lax.psum_scatter(
            partial_rows[2].astype(jnp.bfloat16), "seq", scatter_dimension=1, tiled=True
        ).astype(jnp.float32),
        lax.psum_scatter(
            partial_rows[3].astype(jnp.bfloat16), "seq", scatter_dimension=1, tiled=True
        ).astype(jnp.float32),
        lax.psum_scatter(
            partial_rows[4].astype(jnp.bfloat16), "seq", scatter_dimension=1, tiled=True
        ).astype(jnp.float32),
        lax.psum_scatter(
            partial_rows[5].astype(jnp.bfloat16), "seq", scatter_dimension=1, tiled=True
        ).astype(jnp.float32),
        lax.psum_scatter(
            partial_rows[6].astype(jnp.bfloat16), "seq", scatter_dimension=1, tiled=True
        ).astype(jnp.float32),
        lax.psum_scatter(
            partial_rows[7].astype(jnp.bfloat16), "seq", scatter_dimension=1, tiled=True
        ).astype(jnp.float32),
        lax.psum_scatter(
            partial_rows[8].astype(jnp.bfloat16), "seq", scatter_dimension=1, tiled=True
        ).astype(jnp.float32),
        lax.psum_scatter(
            partial_rows[9].astype(jnp.bfloat16), "seq", scatter_dimension=1, tiled=True
        ).astype(jnp.float32),
        lax.psum_scatter(
            partial_rows[10].astype(jnp.bfloat16), "seq", scatter_dimension=1, tiled=True
        ).astype(jnp.float32),
    )
    token_total = float(row_count * query_len * model_width * device_count)
    sublayer_rms = jnp.sqrt(stat_total / token_total)
    return (
        dec_output,
        encoder_grad,
        decoder_grad,
        sublayer_rms,
        enc_gain1_sum,
        blocks[0],
        blocks[1],
        enc_rel_sum,
        enc_gain2_sum,
        blocks[2],
        blocks[3],
        enc_gainf_sum,
        dec_gain1_sum,
        blocks[4],
        blocks[5],
        dec_rel_sum,
        dec_gain2_sum,
        blocks[6],
        blocks[7],
        blocks[8],
        dec_gain3_sum,
        blocks[9],
        blocks[10],
    )


def solution(mesh):
    placed = (
        P("dp", "seq", None),
        P("dp", "seq", None),
        P("dp", "seq", None),
        P("dp", None),
        P(),
        P(),
        P(),
        P(),
        P(),
        P(),
        P(),
        P(),
        P(),
        P(),
        P(),
        P(),
        P(),
        P(),
        P(),
        P(),
        P(),
        P(),
        P(),
        P(),
    )
    return jax.shard_map(
        on_device,
        mesh=mesh,
        in_specs=placed,
        out_specs=(
            P("dp", "seq", None),
            P("dp", "seq", None),
            P("dp", "seq", None),
            P(),
            P(),
            P("dp", "seq"),
            P("dp", "seq"),
            P(),
            P(),
            P("dp", "seq"),
            P("dp", "seq"),
            P(),
            P(),
            P("dp", "seq"),
            P("dp", "seq"),
            P(),
            P(),
            P("dp", "seq"),
            P("dp", "seq"),
            P("dp", "seq"),
            P(),
            P("dp", "seq"),
            P("dp", "seq"),
        ),
        check_vma=False,
    )
```

profile of v0, /device:TPU:0, one launch (start us, length us, event | category | flops | bytes accessed | tf_op | source)
XLA Modules:
  0.0 1134.1 jit_solution(13294326275058789475)
XLA Ops:
  35.8 20.4 %reshape.1129 = f32[8,256,1279]{2,1,0:T(8,128)} reshape(f32[2619392]{0:T(1024)} %reshape.1174) | data formatting | bytes 20955136 | tf_op jit(solution)/shard_map/reshape | solution.py:68
  71.1 20.7 %reshape.1134 = f32[8,256,1279]{2,1,0:T(8,128)} reshape(f32[2619392]{0:T(1024)} %reshape.1176) | data formatting | bytes 20955136 | tf_op jit(solution)/shard_map/reshape | solution.py:68
  119.6 11.7 %all-gather.15.cloned.1.call-start = ((), (), s32[]{:S(2)}) async-start(), calls=%async_computation.32 | async-start | bytes 1310720 | tf_op jit(solution)/shard_map/all_gather | solution.py:227
  168.8 20.5 %all-gather.15.cloned.1.call-done = bf16[1,1024,512]{2,1,0:T(8,128)(2,1)} async-done(((bf16[1,256,512]{2,1,0:T(8,128)(2,1)}), bf16[1,1024,512]{2,1,0:T(8,128)(2,1)}) %all-gather.15.cloned.1.call-update) | async-done | bytes 1048592 | tf_op jit(solution)/shard_map/all_gather | solution.py:227
  239.7 28.2 %reduce-scatter.45.cloned.1.call-done = bf16[1,256,512]{1,2,0:T(8,128)(2,1)} async-done(((bf16[1,1024,512]{1,2,0:T(8,128)(2,1)}), bf16[1,256,512]{1,2,0:T(8,128)(2,1)}) %reduce-scatter.45.cloned.1.call-update) | async-done | bytes 262160 | tf_op jit(solution)/shard_map/reduce_scatter | solution.py:261
  314.8 30.1 %reduce-scatter.71.cloned.1.call-done = f32[64,512]{1,0:T(8,128)} async-done(((f32[512,512]{1,0:T(8,128)}), f32[64,512]{1,0:T(8,128)}) %reduce-scatter.71.cloned.1.call-update) | async-done | bytes 131088 | tf_op jit(solution)/shard_map/reduce_scatter | solution.py:350
  346.6 37.5 %reduce-scatter.69.cloned.1.call-done = f32[64,512]{1,0:T(8,128)} async-done(((f32[512,512]{1,0:T(8,128)}), f32[64,512]{1,0:T(8,128)}) %reduce-scatter.69.cloned.1.call-update) | async-done | bytes 131088 | tf_op jit(solution)/shard_map/reduce_scatter | solution.py:349
  401.2 21.9 %reduce-scatter.59.cloned.1.call-done = f32[64,512]{1,0:T(8,128)} async-done(((f32[512,512]{1,0:T(8,128)}), f32[64,512]{1,0:T(8,128)}) %reduce-scatter.59.cloned.1.call-update) | async-done | bytes 131088 | tf_op jit(solution)/shard_map/reduce_scatter | solution.py:345
  424.9 27.7 %reduce-scatter.55.cloned.1.call-done = bf16[1,256,512]{1,2,0:T(8,128)(2,1)} async-done(((bf16[1,1024,512]{1,2,0:T(8,128)(2,1)}), bf16[1,256,512]{1,2,0:T(8,128)(2,1)}) %reduce-scatter.55.cloned.1.call-update) | async-done | bytes 262160 | tf_op jit(solution)/shard_map/reduce_scatter | solution.py:287
  452.6 28.1 %reduce-scatter.53.cloned.1.call-done = bf16[1,256,512]{1,2,0:T(8,128)(2,1)} async-done(((bf16[1,1024,512]{1,2,0:T(8,128)(2,1)}), bf16[1,256,512]{1,2,0:T(8,128)(2,1)}) %reduce-scatter.53.cloned.1.call-update) | async-done | bytes 262160 | tf_op jit(solution)/shard_map/reduce_scatter | solution.py:284
  497.7 10.9 reduce-scatter.51.cloned.1.call-done
  508.6 28.1 %reduce-scatter.49.cloned.1.call-done = bf16[1,256,512]{1,2,0:T(8,128)(2,1)} async-done(((bf16[1,1024,512]{1,2,0:T(8,128)(2,1)}), bf16[1,256,512]{1,2,0:T(8,128)(2,1)}) %reduce-scatter.49.cloned.1.call-update) | async-done | bytes 262160 | tf_op jit(solution)/shard_map/reduce_scatter | solution.py:310
  552.9 12.6 %reshape.1180 = bf16[2623488]{0:T(1024)(128)(2,1)} reshape(bf16[8,327936]{1,0:T(8,128)(2,1)} %pad.30) | data formatting | bytes 10493952
  565.5 15.0 %reshape.1154 = bf16[8,256,1281]{2,1,0:T(8,128)(2,1)} reshape(bf16[2623488]{0:T(1024)(128)(2,1)} %reshape.1180) | data formatting | bytes 10493952 | tf_op jit(solution)/shard_map/reshape | solution.py:76
  599.1 41.4 %reduce-scatter.73.cloned.1.call-done = f32[64,1024]{1,0:T(8,128)} async-done(((f32[512,1024]{1,0:T(8,128)}), f32[64,1024]{1,0:T(8,128)}) %reduce-scatter.73.cloned.1.call-update) | async-done | bytes 262160 | tf_op jit(solution)/shard_map/reduce_scatter | solution.py:351
  647.4 47.9 %reduce-scatter.83.cloned.1.call-done = f32[256,512]{1,0:T(8,128)} async-done(((f32[2048,512]{1,0:T(8,128)}), f32[256,512]{1,0:T(8,128)}) %reduce-scatter.83.cloned.1.call-update) | async-done | bytes 524304 | tf_op jit(solution)/shard_map/reduce_scatter | solution.py:354
  708.1 13.2 %reshape.1178 = bf16[2623488]{0:T(1024)(128)(2,1)} reshape(bf16[8,327936]{1,0:T(8,128)(2,1)} %pad.28) | data formatting | bytes 10493952
  721.3 15.2 %reshape.1151 = bf16[8,256,1281]{2,1,0:T(8,128)(2,1)} reshape(bf16[2623488]{0:T(1024)(128)(2,1)} %reshape.1178) | data formatting | bytes 10493952 | tf_op jit(solution)/shard_map/reshape | solution.py:76
  739.8 10.6 reduce-scatter.79.cloned.1.call-done
  759.2 13.2 %reduce-scatter.87.cloned.1.call-done = bf16[128,64]{1,0:T(8,128)(2,1)} async-done(((bf16[512,64]{1,0:T(8,128)(2,1)}), bf16[128,64]{1,0:T(8,128)(2,1)}) %reduce-scatter.87.cloned.1.call-update) | async-done | bytes 16400
  773.2 47.2 %reduce-scatter.67.cloned.1.call-done = f32[64,1536]{1,0:T(8,128)} async-done(((f32[512,1536]{1,0:T(8,128)}), f32[64,1536]{1,0:T(8,128)}) %reduce-scatter.67.cloned.1.call-update) | async-done | bytes 393232 | tf_op jit(solution)/shard_map/reduce_scatter | solution.py:348
  825.0 50.1 %reduce-scatter.65.cloned.1.call-done = f32[256,512]{1,0:T(8,128)} async-done(((f32[2048,512]{1,0:T(8,128)}), f32[256,512]{1,0:T(8,128)}) %reduce-scatter.65.cloned.1.call-update) | async-done | bytes 524304 | tf_op jit(solution)/shard_map/reduce_scatter | solution.py:347
  877.8 39.6 %all-reduce.6 = (f32[8]{0:T(128)S(1)}, f32[3584]{0:T(1024)S(1)}) all-reduce(f32[8]{0:T(128)S(1)} %stack.35, f32[3584]{0:T(1024)S(1)} %constant_dynamic-update-slice_fusion), channel_id=1, replica_groups=mesh['dp'=8,'seq'=4] {'dp','seq'}, use_global_device_ids=true, to_apply=%region_37.38 | all-reduce | flops 3592 | bytes 28736 | tf_op jit(solution)/shard_map/psum | solution.py:245
  917.5 13.1 %reduce-scatter.61.cloned.1.call-done = f32[64,2048]{1,0:T(8,128)} async-done(((f32[512,2048]{1,0:T(8,128)}), f32[64,2048]{1,0:T(8,128)}) %reduce-scatter.61.cloned.1.call-update) | async-done | bytes 524304 | tf_op jit(solution)/shard_map/reduce_scatter | solution.py:346
  934.5 45.5 %reduce-scatter.57.cloned.1.call-done = f32[64,1536]{1,0:T(8,128)} async-done(((f32[512,1536]{1,0:T(8,128)}), f32[64,1536]{1,0:T(8,128)}) %reduce-scatter.57.cloned.1.call-update) | async-done | bytes 393232 | tf_op jit(solution)/shard_map/reduce_scatter | solution.py:344
  984.6 17.5 %reduce-scatter.75.cloned.1.call-done = bf16[64,256]{1,0:T(8,128)(2,1)} async-done(((bf16[64,1024]{1,0:T(8,128)(2,1)}), bf16[64,256]{1,0:T(8,128)(2,1)}) %reduce-scatter.75.cloned.1.call-update) | async-done | bytes 32784 | tf_op jit(solution)/shard_map/reduce_scatter | solution.py:378
  1003.5 18.8 %reduce-scatter.99.cloned.1.call-done = bf16[128,256]{1,0:T(8,128)(2,1)} async-done(((bf16[512,256]{1,0:T(8,128)(2,1)}), bf16[128,256]{1,0:T(8,128)(2,1)}) %reduce-scatter.99.cloned.1.call-update) | async-done | bytes 65552
  1023.9 18.5 %reduce-scatter.81.cloned.1.call-done = bf16[64,512]{1,0:T(8,128)(2,1)} async-done(((bf16[64,2048]{1,0:T(8,128)(2,1)}), bf16[64,512]{1,0:T(8,128)(2,1)}) %reduce-scatter.81.cloned.1.call-update) | async-done | bytes 65552 | tf_op jit(solution)/shard_map/reduce_scatter | solution.py:384
  1043.9 19.7 %reduce-scatter.91.cloned.1.call-done = bf16[384,64]{1,0:T(8,128)(2,1)} async-done(((bf16[1536,64]{1,0:T(8,128)(2,1)}), bf16[384,64]{1,0:T(8,128)(2,1)}) %reduce-scatter.91.cloned.1.call-update) | async-done | bytes 49168
  1065.2 18.7 %reduce-scatter.89.cloned.1.call-done = bf16[128,256]{1,0:T(8,128)(2,1)} async-done(((bf16[512,256]{1,0:T(8,128)(2,1)}), bf16[128,256]{1,0:T(8,128)(2,1)}) %reduce-scatter.89.cloned.1.call-update) | async-done | bytes 65552
  1085.5 18.4 %reduce-scatter.63.cloned.1.call-done = bf16[64,512]{1,0:T(8,128)(2,1)} async-done(((bf16[64,2048]{1,0:T(8,128)(2,1)}), bf16[64,512]{1,0:T(8,128)(2,1)}) %reduce-scatter.63.cloned.1.call-update) | async-done | bytes 65552 | tf_op jit(solution)/shard_map/reduce_scatter | solution.py:363
  1105.4 19.7 %reduce-scatter.85.cloned.1.call-done = bf16[384,64]{1,0:T(8,128)(2,1)} async-done(((bf16[1536,64]{1,0:T(8,128)(2,1)}), bf16[384,64]{1,0:T(8,128)(2,1)}) %reduce-scatter.85.cloned.1.call-update) | async-done | bytes 49168
  (449 shorter events, 336.0 us)
Async XLA Ops:
  7.2 85.7 %all-gather.13.cloned.1.call-start = ((), (), s32[]{:S(2)}) async-start(), calls=%async_computation.31 | async-start | bytes 1310720 | tf_op jit(solution)/shard_map/all_gather | solution.py:197
  12.7 92.6 %all-gather.11.cloned.1.call-start = ((), (), s32[]{:S(2)}) async-start(), calls=%async_computation.30 | async-start | bytes 1310720 | tf_op jit(solution)/shard_map/all_gather | solution.py:198
  13.4 118.0 %all-gather.9.cloned.1.call-start = ((), (), s32[]{:S(2)}) async-start(), calls=%async_computation.29 | async-start | bytes 1310720 | tf_op jit(solution)/shard_map/all_gather | solution.py:215
  17.2 126.4 %all-gather.7.cloned.1.call-start = ((), (), s32[]{:S(2)}) async-start(), calls=%async_computation.28 | async-start | bytes 1310720 | tf_op jit(solution)/shard_map/all_gather | solution.py:216
  17.8 142.7 %all-gather.17.cloned.1.call-start = ((), (), s32[]{:S(2)}) async-start(), calls=%async_computation.33 | async-start | bytes 1310720 | tf_op jit(solution)/shard_map/all_gather | solution.py:226
  152.6 87.1 %reduce-scatter.47.cloned.1.call-start = ((), (), s32[]{:S(2)}) async-start(), calls=%async_computation.35 | async-start | bytes 1310720 | tf_op jit(solution)/shard_map/reduce_scatter | solution.py:264
  225.8 87.2 %reduce-scatter.77.cloned.1.call-start = ((), (), s32[]{:S(2)}) async-start(), calls=%async_computation.50 | async-start | bytes 1179648 | tf_op jit(solution)/shard_map/reduce_scatter | solution.py:352
  227.2 117.7 %reduce-scatter.71.cloned.1.call-start = ((), (), s32[]{:S(2)}) async-start(), calls=%async_computation.47 | async-start | bytes 1179648 | tf_op jit(solution)/shard_map/reduce_scatter | solution.py:350
  232.3 151.7 %reduce-scatter.69.cloned.1.call-start = ((), (), s32[]{:S(2)}) async-start(), calls=%async_computation.46 | async-start | bytes 1179648 | tf_op jit(solution)/shard_map/reduce_scatter | solution.py:349
  234.6 188.5 %reduce-scatter.59.cloned.1.call-start = ((), (), s32[]{:S(2)}) async-start(), calls=%async_computation.41 | async-start | bytes 1179648 | tf_op jit(solution)/shard_map/reduce_scatter | solution.py:345
  276.1 176.5 %reduce-scatter.55.cloned.1.call-start = ((), (), s32[]{:S(2)}) async-start(), calls=%async_computation.39 | async-start | bytes 1310720 | tf_op jit(solution)/shard_map/reduce_scatter | solution.py:287
  282.8 197.8 %reduce-scatter.53.cloned.1.call-start = ((), (), s32[]{:S(2)}) async-start(), calls=%async_computation.38 | async-start | bytes 1310720 | tf_op jit(solution)/shard_map/reduce_scatter | solution.py:284
  294.8 213.8 %reduce-scatter.51.cloned.1.call-start = ((), (), s32[]{:S(2)}) async-start(), calls=%async_computation.37 | async-start | bytes 1310720 | tf_op jit(solution)/shard_map/reduce_scatter | solution.py:313
  301.3 235.4 %reduce-scatter.49.cloned.1.call-start = ((), (), s32[]{:S(2)}) async-start(), calls=%async_computation.36 | async-start | bytes 1310720 | tf_op jit(solution)/shard_map/reduce_scatter | solution.py:310
  312.9 272.5 %reduce-scatter.97.cloned.1.call-start = ((), (), s32[]{:S(2)}) async-start(), calls=%async_computation.60 | async-start | bytes 163840
  314.7 272.2 %reduce-scatter.95.cloned.1.call-start = ((), (), s32[]{:S(2)}) async-start(), calls=%async_computation.59 | async-start | bytes 163840
  346.5 251.1 %reduce-scatter.93.cloned.1.call-start = ((), (), s32[]{:S(2)}) async-start(), calls=%async_computation.58 | async-start | bytes 163840
  385.8 254.7 %reduce-scatter.73.cloned.1.call-start = ((), (), s32[]{:S(2)}) async-start(), calls=%async_computation.48 | async-start | bytes 2359296 | tf_op jit(solution)/shard_map/reduce_scatter | solution.py:351
  389.1 306.1 %reduce-scatter.83.cloned.1.call-start = ((), (), s32[]{:S(2)}) async-start(), calls=%async_computation.53 | async-start | bytes 4718592 | tf_op jit(solution)/shard_map/reduce_scatter | solution.py:354
  392.2 358.2 %reduce-scatter.79.cloned.1.call-start = ((), (), s32[]{:S(2)}) async-start(), calls=%async_computation.51 | async-start | bytes 4718592 | tf_op jit(solution)/shard_map/reduce_scatter | solution.py:353
  396.3 376.0 %reduce-scatter.87.cloned.1.call-start = ((), (), s32[]{:S(2)}) async-start(), calls=%async_computation.55 | async-start | bytes 163840
  424.8 395.6 %reduce-scatter.67.cloned.1.call-start = ((), (), s32[]{:S(2)}) async-start(), calls=%async_computation.45 | async-start | bytes 3538944 | tf_op jit(solution)/shard_map/reduce_scatter | solution.py:348
  484.1 391.0 %reduce-scatter.65.cloned.1.call-start = ((), (), s32[]{:S(2)}) async-start(), calls=%async_computation.44 | async-start | bytes 4718592 | tf_op jit(solution)/shard_map/reduce_scatter | solution.py:347
  488.8 441.7 %reduce-scatter.61.cloned.1.call-start = ((), (), s32[]{:S(2)}) async-start(), calls=%async_computation.42 | async-start | bytes 4718592 | tf_op jit(solution)/shard_map/reduce_scatter | solution.py:346
  492.9 487.1 %reduce-scatter.57.cloned.1.call-start = ((), (), s32[]{:S(2)}) async-start(), calls=%async_computation.40 | async-start | bytes 3538944 | tf_op jit(solution)/shard_map/reduce_scatter | solution.py:344
  540.1 462.0 %reduce-scatter.75.cloned.1.call-start = ((), (), s32[]{:S(2)}) async-start(), calls=%async_computation.49 | async-start | bytes 163840 | tf_op jit(solution)/shard_map/reduce_scatter | solution.py:378
  642.2 380.1 %reduce-scatter.99.cloned.1.call-start = ((), (), s32[]{:S(2)}) async-start(), calls=%async_computation.61 | async-start | bytes 327680
  697.2 345.2 %reduce-scatter.81.cloned.1.call-start = ((), (), s32[]{:S(2)}) async-start(), calls=%async_computation.52 | async-start | bytes 327680 | tf_op jit(solution)/shard_map/reduce_scatter | solution.py:384
  752.1 311.4 %reduce-scatter.91.cloned.1.call-start = ((), (), s32[]{:S(2)}) async-start(), calls=%async_computation.57 | async-start | bytes 491520
  822.4 261.4 %reduce-scatter.89.cloned.1.call-start = ((), (), s32[]{:S(2)}) async-start(), calls=%async_computation.56 | async-start | bytes 327680
  877.1 226.8 %reduce-scatter.63.cloned.1.call-start = ((), (), s32[]{:S(2)}) async-start(), calls=%async_computation.43 | async-start | bytes 327680 | tf_op jit(solution)/shard_map/reduce_scatter | solution.py:363
  932.3 192.8 %reduce-scatter.85.cloned.1.call-start = ((), (), s32[]{:S(2)}) async-start(), calls=%async_computation.54 | async-start | bytes 491520
  (97 other events, 1781.2 us)
Sparse Core Ops, SparseCore 0:
  12.8 30.6 all-gather.12
  45.0 27.4 all-gather.10
  74.6 27.4 all-gather.8
  104.1 27.4 all-gather.6
  133.0 27.4 all-gather.16
  161.8 27.4 all-gather.14
  213.0 26.6 reduce-scatter.46
  242.1 25.7 reduce-scatter.44
  271.0 34.6 reduce-scatter.76
  308.8 36.0 reduce-scatter.70
  348.0 35.9 reduce-scatter.68
  387.1 35.9 reduce-scatter.58
  425.4 27.1 reduce-scatter.54
  454.8 25.7 reduce-scatter.52
  482.8 25.7 reduce-scatter.50
  510.9 25.7 reduce-scatter.48
  539.3 17.8 reduce-scatter.96
  601.1 39.3 reduce-scatter.72
  643.9 51.3 reduce-scatter.82
  699.0 51.3 reduce-scatter.78
  753.2 19.1 reduce-scatter.86
  776.0 44.4 reduce-scatter.66
  823.8 51.3 reduce-scatter.64
  878.7 51.7 reduce-scatter.60
  933.8 46.2 reduce-scatter.56
  982.9 19.1 reduce-scatter.74
  1004.4 17.8 reduce-scatter.98
  1024.5 17.8 reduce-scatter.80
  1044.7 18.8 reduce-scatter.90
  1065.9 17.9 reduce-scatter.88
  1086.0 17.9 reduce-scatter.62
  1106.3 18.8 reduce-scatter.84
  (2 shorter events, 34.6 us)
where the time goes:
time: 1150 us; the launch traced here: 1130 us
  waiting for transfers between devices  655 us (57%)
  local copies, waits for them, and re-layouts  209 us (18%)
  matrix products  141 us (12%)
  other arithmetic  58.5 us (5%)
  blocking collectives  39.6 us (3%)
  between operations  16.4 us (1%)
  starting transfers between devices  13.9 us (1%)
    unnamed x42, waiting for transfers between devices  101 us
    unnamed x223, local copies, waits for them, and re-layouts  95.5 us
    reduce_scatter x1, waiting for transfers between devices, on_device(): lax.psum_scatter(enc_wo_grad, 'dp', scatter_dimension=0, tiled=True)  50.1 us
    reduce_scatter x1, waiting for transfers between devices, on_device(): lax.psum_scatter(dec_wo_grad, 'dp', scatter_dimension=0, tiled=True)  47.9 us
    reduce_scatter x1, waiting for transfers between devices, on_device(): lax.psum_scatter(dec_qkv_grad, 'dp', scatter_dimension=0, tiled=True)  47.2 us
    reduce_scatter x1, waiting for transfers between devices, on_device(): lax.psum_scatter(enc_qkv_grad, 'dp', scatter_dimension=0, tiled=True)  45.5 us
    reduce_scatter x1, waiting for transfers between devices, on_device(): lax.psum_scatter(cross_kv_grad, 'dp', scatter_dimension=0, tiled=True)  41.4 us
    reshape x2, local copies, waits for them, and re-layouts, position_bias(): return trimmed.reshape(-1, row_count, width_all)[:, :, :length]  41.1 us
  transfers between devices with their start and end apart: 34, of which 27 were waited for; matrix products, arithmetic and copies ran while one was open for 32% of the time, Pallas kernels for 0%

commit v1 on v0

v1 whole, which is shorter than its diff:
```python
from functools import partial

import jax
import jax.numpy as jnp
from jax import lax
from jax.sharding import PartitionSpec as P

HEAD_DIM = 64
BF = jnp.bfloat16
F32 = jnp.float32

eps_norm = 1e-06
negative = -1000000000.0


def rms_norm(values, gain_vec):
    return (
        values * lax.rsqrt(jnp.mean(values * values, axis=-1, keepdims=True) + eps_norm) * gain_vec
    )


def norm_back(values, gain_vec, incoming):
    _, pull = jax.vjp(rms_norm, values, gain_vec)
    return pull(incoming)


def gelu_back(hidden, incoming):
    _, pull = jax.vjp(partial(jax.nn.gelu, approximate=True), hidden)
    return pull(incoming)[0]


def dense(acts, weight):
    return jnp.dot(acts, weight, preferred_element_type=F32)


def dense_back(incoming, weight):
    return lax.dot_general(
        incoming, weight, (((1,), (1,)), ((), ())), preferred_element_type=F32
    )


def weight_grad(acts, incoming):
    return lax.dot_general(acts, incoming, (((0,), (0,)), ((), ())), preferred_element_type=F32)


def split_heads(tensor):
    return tensor.reshape(tensor.shape[0], -1, HEAD_DIM)


def segment_ids(lengths_row, length):
    places = jnp.arange(length, dtype=jnp.int32)
    total = jnp.zeros((length,), jnp.int32)
    end = jnp.int32(0)
    for slot in range(lengths_row.shape[0]):
        end = end + lengths_row[slot]
        total = total + (places >= end).astype(jnp.int32)
    return total


def bucket_onehot(lookup, first_pos, row_count, length, bucket_count):
    width_all = length + row_count - 1
    window = lax.dynamic_slice_in_dim(lookup, length - first_pos - row_count, width_all)
    return (window[:, None] == jnp.arange(bucket_count, dtype=jnp.int32)[None, :]).astype(F32)


def position_bias(rel_table, lookup, first_pos, row_count, length):
    onehot = bucket_onehot(lookup, first_pos, row_count, length, rel_table.shape[0])
    width_all = length + row_count - 1
    per_offset = jnp.dot(onehot, rel_table, precision=lax.Precision.HIGHEST).T
    padded = jnp.pad(per_offset, ((0, 0), (0, 1)))
    repeated = jnp.tile(padded, (1, row_count))
    trimmed = repeated[:, row_count - 1 : row_count - 1 + row_count * width_all]
    return trimmed.reshape(-1, row_count, width_all)[:, :, :length]


def bias_grad(grad_sum, lookup, first_pos, bucket_count):
    head_count, row_count, length = grad_sum.shape
    width_all = length + row_count - 1
    padded = jnp.pad(grad_sum, ((0, 0), (0, 0), (0, row_count)))
    flat_grad = jnp.pad(padded.reshape(head_count, -1), ((0, 0), (row_count - 1, 1)))
    skewed = flat_grad.reshape(head_count, row_count, length + row_count + 1)[:, :, :width_all]
    per_offset = jnp.sum(skewed, axis=1)
    onehot = bucket_onehot(lookup, first_pos, row_count, length, bucket_count)
    return jnp.dot(onehot.T, per_offset.T, precision=lax.Precision.HIGHEST)


def raw_scores(queries, key_rows, pos_bias, allowed):
    scores = jnp.einsum(
        "qhd,khd->hqk", split_heads(queries), split_heads(key_rows), preferred_element_type=F32
    )
    if pos_bias is not None:
        scores = scores + pos_bias
    return jnp.where(allowed[None], scores, negative)


def attend_fwd(queries, key_rows, values, pos_bias, allowed):
    scores = raw_scores(queries, key_rows, pos_bias, allowed)
    row_max = jnp.max(scores, axis=-1, keepdims=True)
    exponent = jnp.exp(scores - row_max)
    row_sum = jnp.sum(exponent, axis=-1, keepdims=True)
    probs_low = (exponent / row_sum).astype(BF)
    mixed = jnp.einsum("hqk,khd->qhd", probs_low, split_heads(values), preferred_element_type=F32)
    return (mixed.reshape(queries.shape), row_max + jnp.log(row_sum))


def attend_back(queries, key_rows, values, pos_bias, allowed, log_total, incoming):
    scores = raw_scores(queries, key_rows, pos_bias, allowed)
    probs_f = jnp.exp(scores - log_total)
    grad_heads = split_heads(incoming)
    grad_values = jnp.einsum(
        "hqk,qhd->khd", probs_f.astype(BF), grad_heads, preferred_element_type=F32
    )
    grad_probs = jnp.einsum(
        "qhd,khd->hqk", grad_heads, split_heads(values), preferred_element_type=F32
    )
    grad_scores = (
        probs_f * (grad_probs - jnp.sum(probs_f * grad_probs, axis=-1, keepdims=True))
    ).astype(BF)
    grad_queries = jnp.einsum(
        "hqk,khd->qhd", grad_scores, split_heads(key_rows), preferred_element_type=F32
    )
    grad_keys = jnp.einsum(
        "hqk,qhd->khd", grad_scores, split_heads(queries), preferred_element_type=F32
    )
    return (
        grad_queries.reshape(queries.shape),
        grad_keys.reshape(key_rows.shape),
        grad_values.reshape(key_rows.shape),
        grad_scores.astype(F32),
    )


def flip(value, axis, bit):
    count = lax.axis_size(axis)
    return lax.ppermute(value, axis, [(i, i ^ bit) for i in range(count)])


def swap_rows(value):
    dp, seq = lax.axis_size("dp"), lax.axis_size("seq")
    half = seq // 2
    pairs = []
    for d in range(dp):
        for s in range(seq):
            if (d & 1) != (s >= half):
                pairs.append((d * seq + s, (d ^ 1) * seq + (s ^ half)))
    return lax.ppermute(value, ("dp", "seq"), pairs)


def gather_row(own):
    other = flip(own, "seq", 1)
    core_own = flip(own, "dp", 1)
    core_other = flip(other, "dp", 1)
    return [own, other, core_own, core_other]


def scatter_row(parts):
    low = [part.astype(BF) for part in parts]
    got = flip(jnp.stack([low[2], low[3]]), "dp", 1).astype(F32)
    mine = parts[0] + got[0]
    theirs = (parts[1] + got[1]).astype(BF)
    return mine + flip(theirs, "seq", 1).astype(F32)


def natural(parts, quarter):
    rel = jnp.stack(parts)
    return jnp.concatenate(
        [lax.dynamic_index_in_dim(rel, quarter ^ b, 0, keepdims=False) for b in range(4)]
    )


def relative(whole, quarter):
    nat = whole.reshape(4, -1, whole.shape[-1])
    return [lax.dynamic_index_in_dim(nat, quarter ^ b, 0, keepdims=False) for b in range(4)]


def reduce_weight(grad, late_first):
    dp, seq = lax.axis_size("dp"), lax.axis_size("seq")
    bits = dp.bit_length() - 1
    rows, cols = grad.shape
    order = [0] + (list(range(bits - 1, 0, -1)) if late_first else list(range(1, bits)))
    me = lax.axis_index("dp")
    now = grad.astype(BF).reshape([2] * bits + [rows // dp, cols])
    left = list(range(bits - 1, -1, -1))
    for bit in order:
        axis = left.index(bit)
        mine = (me >> bit) & 1
        keep = lax.dynamic_index_in_dim(now, mine, axis, keepdims=False)
        send = lax.dynamic_index_in_dim(now, 1 - mine, axis, keepdims=False)
        left.pop(axis)
        total = keep.astype(F32) + flip(send, "dp", 1 << bit).astype(F32)
        now = total.astype(BF)
    me = lax.axis_index("seq")
    width = cols
    total = now.astype(F32)
    for step in (seq // 2, 1):
        width = width // 2
        mine = jnp.where((me & step) != 0, 1, 0)
        keep = lax.dynamic_slice_in_dim(total, mine * width, width, 1)
        send = lax.dynamic_slice_in_dim(total, (1 - mine) * width, width, 1).astype(BF)
        total = keep + flip(send, "seq", step).astype(F32)
    return total


def all_sum(flat):
    for bit in range(lax.axis_size("dp").bit_length() - 1):
        flat = flat + flip(flat, "dp", 1 << bit)
    for bit in range(lax.axis_size("seq").bit_length() - 1):
        flat = flat + flip(flat, "seq", 1 << bit)
    return flat


def flatten_all(members):
    return jnp.concatenate([member.reshape(-1) for member in members])


def unflatten(flat_grad, members):
    result = []
    offset = 0
    for member in members:
        result.append(flat_grad[offset : offset + member.size].reshape(member.shape))
        offset += member.size
    return result


def on_device(
    encoder_input,
    decoder_input,
    output_grad,
    segment_lengths,
    bucket_table,
    enc_gain1,
    enc_qkv,
    enc_proj,
    enc_rel,
    enc_gain2,
    enc_wi,
    enc_wo,
    enc_gainf,
    dec_gain1,
    dec_qkv,
    dec_proj,
    dec_rel,
    dec_gain2,
    cross_q,
    cross_kv,
    cross_proj,
    dec_gain3,
    dec_wi,
    dec_wo,
):
    seq_count = lax.axis_size("seq")
    device_count = lax.axis_size(("dp", "seq"))
    _, query_len, model_width = encoder_input.shape
    full_len = query_len * seq_count
    core = lax.axis_index("dp") & 1
    place = lax.axis_index("seq")
    moved = core != (place // 2)
    quarter = (place & 1) + 2 * core
    first_pos = quarter * query_len
    inner = enc_proj.shape[0]
    bucket_count = enc_rel.shape[0]

    def bring(value):
        return jnp.where(moved, swap_rows(value), value)

    lengths = bring(segment_lengths)[0]
    enc_own = bring(encoder_input[0])
    enc_all = natural(gather_row(enc_own), quarter)
    dec_own = bring(decoder_input[0])
    dec_all = natural(gather_row(dec_own), quarter)
    top_low = bring(output_grad[0])

    ids_full = segment_ids(lengths, full_len)
    ids_own = lax.dynamic_slice_in_dim(ids_full, first_pos, query_len)
    same_seg = ids_own[:, None] == ids_full[None, :]
    key_pos = jnp.arange(full_len, dtype=jnp.int32)
    query_pos = first_pos + jnp.arange(query_len, dtype=jnp.int32)
    causal = same_seg & (key_pos[None, :] <= query_pos[:, None])
    enc_bias = position_bias(enc_rel, bucket_table, first_pos, query_len, full_len)
    dec_bias = position_bias(dec_rel, bucket_table, first_pos, query_len, full_len)

    enc_in = enc_own.astype(F32)
    enc_a_all = rms_norm(enc_all.astype(F32), enc_gain1).astype(BF)
    enc_a = rms_norm(enc_in, enc_gain1).astype(BF)
    enc_query = dense(enc_a, enc_qkv[:, :inner]).astype(BF)
    enc_pair = dense(enc_a_all, enc_qkv[:, inner:]).astype(BF)
    enc_keys, enc_vals = enc_pair[:, :inner], enc_pair[:, inner:]
    enc_mix, enc_lse = attend_fwd(enc_query, enc_keys, enc_vals, enc_bias, same_seg)
    enc_mix_low = enc_mix.astype(BF)
    enc_att = dense(enc_mix_low, enc_proj)
    enc_h1 = enc_in + enc_att
    enc_b = rms_norm(enc_h1, enc_gain2).astype(BF)
    enc_u = dense(enc_b, enc_wi)
    enc_g = jax.nn.gelu(enc_u, approximate=True).astype(BF)
    enc_ffn = dense(enc_g, enc_wo)
    enc_h2 = enc_h1 + enc_ffn
    encoded = rms_norm(enc_h2, enc_gainf).astype(BF)
    encoded_all = natural(gather_row(encoded), quarter)

    dec_in = dec_own.astype(F32)
    dec_a_all = rms_norm(dec_all.astype(F32), dec_gain1).astype(BF)
    dec_a = rms_norm(dec_in, dec_gain1).astype(BF)
    dec_query = dense(dec_a, dec_qkv[:, :inner]).astype(BF)
    dec_pair = dense(dec_a_all, dec_qkv[:, inner:]).astype(BF)
    dec_keys, dec_vals = dec_pair[:, :inner], dec_pair[:, inner:]
    dec_mix, dec_lse = attend_fwd(dec_query, dec_keys, dec_vals, dec_bias, causal)
    dec_mix_low = dec_mix.astype(BF)
    dec_att = dense(dec_mix_low, dec_proj)
    dec_h1 = dec_in + dec_att
    dec_c = rms_norm(dec_h1, dec_gain2).astype(BF)
    cross_query = dense(dec_c, cross_q).astype(BF)

    cross_pair = dense(encoded_all, cross_kv).astype(BF)
    cross_keys, cross_vals = cross_pair[:, :inner], cross_pair[:, inner:]
    cross_mix, cross_lse = attend_fwd(cross_query, cross_keys, cross_vals, None, same_seg)
    cross_mix_low = cross_mix.astype(BF)
    cross_att = dense(cross_mix_low, cross_proj)
    dec_h2 = dec_h1 + cross_att
    dec_b = rms_norm(dec_h2, dec_gain3).astype(BF)
    dec_u = dense(dec_b, dec_wi)
    dec_g = jax.nn.gelu(dec_u, approximate=True).astype(BF)
    dec_ffn = dense(dec_g, dec_wo)
    dec_h3 = dec_h2 + dec_ffn
    dec_output = bring(dec_h3.astype(BF))
    stat_terms = jnp.stack(
        [
            jnp.sum(member * member)
            for member in (enc_att, enc_h1, enc_ffn, enc_h2, dec_att, cross_att, dec_ffn, dec_h3)
        ]
    )

    top_grad = top_low.astype(F32)
    dec_wo_grad = weight_grad(dec_g, top_low)
    dec_u_grad = gelu_back(dec_u, dense_back(top_low, dec_wo)).astype(BF)
    dec_wi_grad = weight_grad(dec_b, dec_u_grad)
    dec_h2_part, dec_gain3_grad = norm_back(dec_h2, dec_gain3, dense_back(dec_u_grad, dec_wi))
    dec_h2_grad = top_grad + dec_h2_part
    cross_att_grad = dec_h2_grad.astype(BF)
    cross_proj_grad = weight_grad(cross_mix_low, cross_att_grad)
    cross_mix_grad = dense_back(cross_att_grad, cross_proj).astype(BF)
    cross_q_part, cross_k_part, cross_v_part, _ = attend_back(
        cross_query, cross_keys, cross_vals, None, same_seg, cross_lse, cross_mix_grad
    )
    cross_pair_grad = jnp.concatenate([cross_k_part, cross_v_part], axis=-1).astype(BF)
    encoded_grad = scatter_row(relative(dense_back(cross_pair_grad, cross_kv), quarter))
    cross_query_grad = cross_q_part.astype(BF)
    cross_q_grad = weight_grad(dec_c, cross_query_grad)
    cross_kv_grad = weight_grad(encoded_all, cross_pair_grad)
    dec_h1_part, dec_gain2_grad = norm_back(
        dec_h1, dec_gain2, dense_back(cross_query_grad, cross_q)
    )
    dec_h1_grad = dec_h2_grad + dec_h1_part
    dec_att_grad = dec_h1_grad.astype(BF)
    dec_proj_grad = weight_grad(dec_mix_low, dec_att_grad)
    dec_mix_grad = dense_back(dec_att_grad, dec_proj).astype(BF)
    dec_q_part, dec_k_part, dec_v_part, dec_bias_sum = attend_back(
        dec_query, dec_keys, dec_vals, dec_bias, causal, dec_lse, dec_mix_grad
    )
    dec_query_grad = dec_q_part.astype(BF)
    dec_pair_grad = jnp.concatenate([dec_k_part, dec_v_part], axis=-1).astype(BF)
    dec_qkv_grad = jnp.concatenate(
        [weight_grad(dec_a, dec_query_grad), weight_grad(dec_a_all, dec_pair_grad)], axis=1
    )
    dec_a_parts = relative(dense_back(dec_pair_grad, dec_qkv[:, inner:]), quarter)
    dec_a_parts[0] = dec_a_parts[0] + dense_back(dec_query_grad, dec_qkv[:, :inner])
    dec_in_part, dec_gain1_grad = norm_back(dec_in, dec_gain1, scatter_row(dec_a_parts))
    decoder_grad = bring((dec_h1_grad + dec_in_part).astype(BF))
    dec_rel_grad = bias_grad(dec_bias_sum, bucket_table, first_pos, bucket_count)

    enc_h2_grad, enc_gainf_grad = norm_back(enc_h2, enc_gainf, encoded_grad)
    enc_ffn_grad = enc_h2_grad.astype(BF)
    enc_wo_grad = weight_grad(enc_g, enc_ffn_grad)
    enc_u_grad = gelu_back(enc_u, dense_back(enc_ffn_grad, enc_wo)).astype(BF)
    enc_wi_grad = weight_grad(enc_b, enc_u_grad)
    enc_h1_part, enc_gain2_grad = norm_back(enc_h1, enc_gain2, dense_back(enc_u_grad, enc_wi))
    enc_h1_grad = enc_h2_grad + enc_h1_part
    enc_att_grad = enc_h1_grad.astype(BF)
    enc_proj_grad = weight_grad(enc_mix_low, enc_att_grad)
    enc_mix_grad = dense_back(enc_att_grad, enc_proj).astype(BF)
    enc_q_part, enc_k_part, enc_v_part, enc_bias_sum = attend_back(
        enc_query, enc_keys, enc_vals, enc_bias, same_seg, enc_lse, enc_mix_grad
    )
    enc_query_grad = enc_q_part.astype(BF)
    enc_pair_grad = jnp.concatenate([enc_k_part, enc_v_part], axis=-1).astype(BF)
    enc_qkv_grad = jnp.concatenate(
        [weight_grad(enc_a, enc_query_grad), weight_grad(enc_a_all, enc_pair_grad)], axis=1
    )
    enc_a_parts = relative(dense_back(enc_pair_grad, enc_qkv[:, inner:]), quarter)
    enc_a_parts[0] = enc_a_parts[0] + dense_back(enc_query_grad, enc_qkv[:, :inner])
    enc_in_part, enc_gain1_grad = norm_back(enc_in, enc_gain1, scatter_row(enc_a_parts))
    encoder_grad = bring((enc_h1_grad + enc_in_part).astype(BF))
    enc_rel_grad = bias_grad(enc_bias_sum, bucket_table, first_pos, bucket_count)

    small_members = [
        stat_terms,
        enc_gain1_grad,
        enc_rel_grad,
        enc_gain2_grad,
        enc_gainf_grad,
        dec_gain1_grad,
        dec_rel_grad,
        dec_gain2_grad,
        dec_gain3_grad,
    ]
    flat = flatten_all(small_members)
    flat = jnp.pad(flat, (0, -flat.size % 1024)).reshape(-1, 128)
    (
        stat_total,
        enc_gain1_sum,
        enc_rel_sum,
        enc_gain2_sum,
        enc_gainf_sum,
        dec_gain1_sum,
        dec_rel_sum,
        dec_gain2_sum,
        dec_gain3_sum,
    ) = unflatten(all_sum(flat).reshape(-1), small_members)
    blocks = [
        reduce_weight(grad, late)
        for grad, late in (
            (dec_wo_grad, False),
            (dec_wi_grad, True),
            (cross_proj_grad, False),
            (cross_q_grad, False),
            (cross_kv_grad, True),
            (dec_proj_grad, False),
            (dec_qkv_grad, True),
            (enc_wo_grad, False),
            (enc_wi_grad, True),
            (enc_proj_grad, False),
            (enc_qkv_grad, True),
        )
    ]
    token_total = float(query_len * model_width * device_count)
    sublayer_rms = jnp.sqrt(stat_total / token_total)
    return (
        dec_output[None],
        encoder_grad[None],
        decoder_grad[None],
        sublayer_rms,
        enc_gain1_sum,
        blocks[10],
        blocks[9],
        enc_rel_sum,
        enc_gain2_sum,
        blocks[8],
        blocks[7],
        enc_gainf_sum,
        dec_gain1_sum,
        blocks[6],
        blocks[5],
        dec_rel_sum,
        dec_gain2_sum,
        blocks[3],
        blocks[4],
        blocks[2],
        dec_gain3_sum,
        blocks[1],
        blocks[0],
    )


def solution(mesh):
    rows = P("dp", "seq", None)
    both = P("dp", "seq")
    return jax.shard_map(
        on_device,
        mesh=mesh,
        in_specs=(rows, rows, rows, P("dp", None)) + (P(),) * 20,
        out_specs=(
            (rows,) * 3
            + (P(),) * 2
            + (both,) * 2
            + (P(),) * 2
            + (both,) * 2
            + (P(),) * 2
            + (both,) * 2
            + (P(),) * 2
            + (both,) * 3
            + (P(),)
            + (both,) * 2
        ),
        check_vma=False,
    )
```

time: 1150 us -> 616 us (0.54)
  waiting for transfers between devices: 655 us -> 119 us
  starting transfers between devices: 13.9 us -> 106 us
  blocking collectives: 39.6 us -> 0 us
  matrix products: 141 us -> 111 us
  local copies, waits for them, and re-layouts: 209 us -> 190 us
  other arithmetic: 58.5 us -> 74.1 us
    reduce_scatter x20 -> x0, waiting for transfers between devices: 528 us -> none  [the longest x1 50.1 us: on_device(): lax.psum_scatter(enc_wo_grad, 'dp', scatter_dimension=0, tiled=True)]
    ppermute x0 -> x82, waiting for transfers between devices: none -> 119 us  [the longest x75 119 us: flip(): return lax.ppermute(value, axis, [(i, i ^ bit) for i in range(count)])]
    ppermute x0 -> x82, starting transfers between devices: none -> 106 us  [the longest x75 97.8 us: flip(): return lax.ppermute(value, axis, [(i, i ^ bit) for i in range(count)])]
    unnamed x42 -> x0, waiting for transfers between devices: 101 us -> none
    psum x1 -> x0, blocking collectives: 39.6 us -> none  [on_device(): stat_total = lax.psum(stat_terms, ('dp', 'seq'))]
    dot_general x51 -> x57, matrix products: 138 us -> 108 us  [the longest x13 19.5 us: weight_grad(): lax.dot_general(acts, incoming, (((0,), (0,)), ((), ())), preferred_eleme...]
    unnamed x223 -> x328, local copies, waits for them, and re-layouts: 95.5 us -> 66.4 us
    all_gather x6 -> x0, waiting for transfers between devices: 26.8 us -> none  [the longest x1 20.5 us: on_device(): lax.all_gather(cross_pair[..., inner_width:], 'seq', axis=1, tiled=True)]
  transfers between devices with their start and end apart: 34 -> 82, of which waited for: 27 -> 38; matrix products, arithmetic and copies ran while one was open for 32% -> 46% of each run, Pallas kernels for 0% -> 0%
where the time goes in v1:
time: 616 us; the launch traced here: 606 us
  local copies, waits for them, and re-layouts  190 us (31%)
  waiting for transfers between devices  119 us (19%)
  matrix products  111 us (18%)
  starting transfers between devices  106 us (17%)
  other arithmetic  74.1 us (12%)
  between operations  6.55 us (1%)
    ppermute x75, waiting for transfers between devices, flip(): return lax.ppermute(value, axis, [(i, i ^ bit) for i in range(count)])  119 us
    ppermute x75, starting transfers between devices, flip(): return lax.ppermute(value, axis, [(i, i ^ bit) for i in range(count)])  97.8 us
    unnamed x328, local copies, waits for them, and re-layouts  66.4 us
    reshape x2, local copies, waits for them, and re-layouts, position_bias(): return trimmed.reshape(-1, row_count, width_all)[:, :, :length]  40.9 us
    reshape x2, local copies, waits for them, and re-layouts, bias_grad(): flat_grad.reshape(head_count, row_count, length + row_count + 1)  29.9 us
    dot_general x13, matrix products, weight_grad(): lax.dot_general(acts, incoming, (((0,), (0,)), ((), ())), preferred_eleme...  19.5 us
    dot_general x13, matrix products, dense_back(): lax.dot_general(incoming, weight, (((1,), (1,)), ((), ())), preferred_ele...  19.1 us
    dot_general x13, matrix products, dense(): return jnp.dot(acts, weight, preferred_element_type=F32)  17.2 us
  transfers between devices with their start and end apart: 82, of which 38 were waited for; matrix products, arithmetic and copies ran while one was open for 46% of the time, Pallas kernels for 0%

profile of v1, /device:TPU:0, one launch (start us, length us, event | category | flops | bytes accessed | tf_op | source)
XLA Modules:
  0.0 606.1 jit_solution(10500680258021481861)
XLA Ops:
  7.6 5.5 slice.167
  13.1 8.5 %reshape.647 = f32[2619392]{0:T(1024)} reshape(f32[8,327424]{1,0:T(8,128)} %slice.167) | data formatting | bytes 20955136
  21.6 20.3 %reshape.577 = f32[8,256,1279]{2,1,0:T(8,128)} reshape(f32[2619392]{0:T(1024)} %reshape.647) | data formatting | bytes 20955136 | tf_op jit(solution)/shard_map/reshape | solution.py:73
  43.2 5.6 slice.163
  48.8 8.5 %reshape.645 = f32[2619392]{0:T(1024)} reshape(f32[8,327424]{1,0:T(8,128)} %slice.163) | data formatting | bytes 20955136
  57.3 20.5 %reshape.573 = f32[8,256,1279]{2,1,0:T(8,128)} reshape(f32[2619392]{0:T(1024)} %reshape.645) | data formatting | bytes 20955136 | tf_op jit(solution)/shard_map/reshape | solution.py:73
  86.2 9.7 %collective-permute-start.7 = (bf16[256,512]{1,0:T(8,128)(2,1)S(1)}, bf16[256,512]{1,0:T(8,128)(2,1)}, u32[]{:S(2)}, u32[]{:S(2)}) collective-permute-start(bf16[256,512]{1,0:T(8,128)(2,1)S(1)} %get-tuple-element.74), channel_id=1, source_target_pairs={{0,4},{4,0},{8,12},{12,8},{16,20},{20,16},{24,28},{28,24},{1,5},{5... | collective-permute-start | bytes 786440 | tf_op jit(solution)/shard_map/ppermute | solution.py:135
  110.3 5.9 fusion.216
  131.3 4.9 collective-permute-done.9
  179.6 5.7 multiply_reduce_fusion.2
  185.3 6.3 %fusion.54 = bf16[8,64,1024]{2,1,0:T(8,128)(2,1)} fusion(bf16[256,8,64]{0,2,1:T(8,128)(2,1)S(1)} %bitcast.505, f32[8,256,1024]{2,1,0:T(8,128)} %copy-done.4, f32[8,256]{1,0:T(8,128)S(1)} %log_add_fusion.2, pred[256,1024]{1,0:T(8,128)(4,1)S(1)} %get-tuple-element.130), kind=kOutput, calls=%fused_computation.111 | convolution fusion | flops 275251200 | bytes 9969664 | tf_op jit(solution)/shard_map/hqk,qhd->khd/dot_general | solution.py:110
  191.7 4.6 multiply_convert_fusion.2
  203.4 5.4 multiply_reduce_fusion
  239.7 12.6 %reshape.651 = bf16[2623488]{0:T(1024)(128)(2,1)} reshape(bf16[8,327936]{1,0:T(8,128)(2,1)} %pad.34) | data formatting | bytes 10493952
  252.3 14.9 %reshape.597 = bf16[8,256,1281]{2,1,0:T(8,128)(2,1)} reshape(bf16[2623488]{0:T(1024)(128)(2,1)} %reshape.651) | data formatting | bytes 10493952 | tf_op jit(solution)/shard_map/reshape | solution.py:81
  275.8 8.2 %collective-permute-start.57 = (bf16[2,2,64,512]{3,2,0,1:T(8,128)(2,1)S(1)}, bf16[2,2,64,512]{3,2,0,1:T(8,128)(2,1)S(1)}, u32[]{:S(2)}, u32[]{:S(2)}) collective-permute-start(bf16[2,2,64,512]{3,2,0,1:T(8,128)(2,1)S(1)} %bitcast.547), channel_id=1, source_target_pairs={{0,4},{4,0},{8,12},{12,8},{16,20},{20,16},{24,28},{28,24},{1,5},{5... | collective-permute-start | bytes 786440 | tf_op jit(solution)/shard_map/ppermute | solution.py:135
  316.6 4.1 collective-permute-done.70
  321.5 4.0 collective-permute-done.60
  326.3 4.0 collective-permute-done.55
  359.7 5.3 multiply_reduce_fusion.1
  403.6 12.7 %reshape.649 = bf16[2623488]{0:T(1024)(128)(2,1)} reshape(bf16[8,327936]{1,0:T(8,128)(2,1)} %pad.32) | data formatting | bytes 10493952
  416.3 15.1 %reshape.594 = bf16[8,256,1281]{2,1,0:T(8,128)(2,1)} reshape(bf16[2623488]{0:T(1024)(128)(2,1)} %reshape.649) | data formatting | bytes 10493952 | tf_op jit(solution)/shard_map/reshape | solution.py:81
  466.2 3.8 collective-permute-start.35
  481.9 8.7 %collective-permute-done.73 = bf16[2,64,2048]{2,1,0:T(8,128)(2,1)S(1)} collective-permute-done((bf16[2,64,2048]{2,1,0:T(8,128)(2,1)S(1)}, bf16[2,64,2048]{2,1,0:T(8,128)(2,1)S(1)}, u32[]{:S(2)}, u32[]{:S(2)}) %collective-permute-start.73) | collective-permute-done | bytes 524320 | tf_op jit(solution)/shard_map/ppermute | solution.py:135
  495.7 5.3 concatenate.44
  527.2 4.3 collective-permute-start.80
  536.2 11.2 %collective-permute-done.80 = bf16[256,256]{1,0:T(8,128)(2,1)S(1)} collective-permute-done((bf16[256,256]{1,0:T(8,128)(2,1)S(1)}, bf16[256,256]{1,0:T(8,128)(2,1)S(1)}, u32[]{:S(2)}, u32[]{:S(2)}) %collective-permute-start.80) | collective-permute-done | bytes 131104 | tf_op jit(solution)/shard_map/ppermute | solution.py:135
  551.0 6.1 collective-permute-done.49
  559.0 4.2 collective-permute-start.50
  575.2 5.3 collective-permute-done.44
  583.8 5.3 collective-permute-done.45
  596.3 4.5 collective-permute-done.30
  (744 shorter events, 348.7 us)
Async XLA Ops:
  0.7 82.2 %collective-permute-start.5 = (bf16[256,512]{1,0:T(8,128)(2,1)}, bf16[256,512]{1,0:T(8,128)(2,1)}, u32[]{:S(2)}, u32[]{:S(2)}) collective-permute-start(bf16[256,512]{1,0:T(8,128)(2,1)} %bitcast.544), channel_id=1, source_target_pairs={{2,4},{3,5},{4,2},{5,3},{10,12},{11,13},{12,10},{13,11},{18,20},{1... | collective-permute-start | bytes 786440 | tf_op jit(solution)/shard_map/ppermute | solution.py:146
  2.2 75.7 %collective-permute-start.4 = (s32[1,4]{1,0:T(1,128)}, s32[1,4]{1,0:T(1,128)S(1)}, u32[]{:S(2)}, u32[]{:S(2)}) collective-permute-start(s32[1,4]{1,0:T(1,128)} %param.27), channel_id=1, source_target_pairs={{2,4},{3,5},{4,2},{5,3},{10,12},{11,13},{12,10},{13,11},{18,20},{1... | collective-permute-start | bytes 56 | tf_op jit(solution)/shard_map/ppermute | solution.py:146
  2.8 93.0 %collective-permute-start = (bf16[256,512]{1,0:T(8,128)(2,1)}, bf16[256,512]{1,0:T(8,128)(2,1)S(1)}, u32[]{:S(2)}, u32[]{:S(2)}) collective-permute-start(bf16[256,512]{1,0:T(8,128)(2,1)} %bitcast.545), channel_id=1, source_target_pairs={{2,4},{3,5},{4,2},{5,3},{10,12},{11,13},{12,10},{13,11},{18,20},{1... | collective-permute-start | bytes 786440 | tf_op jit(solution)/shard_map/ppermute | solution.py:146
  3.5 125.2 %collective-permute-start.13 = (bf16[256,512]{1,0:T(8,128)(2,1)}, bf16[256,512]{1,0:T(8,128)(2,1)}, u32[]{:S(2)}, u32[]{:S(2)}) collective-permute-start(bf16[256,512]{1,0:T(8,128)(2,1)} %bitcast.548), channel_id=1, source_target_pairs={{2,4},{3,5},{4,2},{5,3},{10,12},{11,13},{12,10},{13,11},{18,20},{1... | collective-permute-start | bytes 786440 | tf_op jit(solution)/shard_map/ppermute | solution.py:146
  83.1 14.9 %collective-permute-start.6 = (bf16[256,512]{1,0:T(8,128)(2,1)S(1)}, bf16[256,512]{1,0:T(8,128)(2,1)}, u32[]{:S(2)}, u32[]{:S(2)}) collective-permute-start(bf16[256,512]{1,0:T(8,128)(2,1)S(1)} %get-tuple-element.74), channel_id=1, source_target_pairs={{0,1},{1,0},{2,3},{3,2},{4,5},{5,4},{6,7},{7,6},{8,9},{9,8},{10,11... | collective-permute-start | bytes 786440 | tf_op jit(solution)/shard_map/ppermute | solution.py:135
  86.2 19.4 %collective-permute-start.7 = (bf16[256,512]{1,0:T(8,128)(2,1)S(1)}, bf16[256,512]{1,0:T(8,128)(2,1)}, u32[]{:S(2)}, u32[]{:S(2)}) collective-permute-start(bf16[256,512]{1,0:T(8,128)(2,1)S(1)} %get-tuple-element.74), channel_id=1, source_target_pairs={{0,4},{4,0},{8,12},{12,8},{16,20},{20,16},{24,28},{28,24},{1,5},{5... | collective-permute-start | bytes 786440 | tf_op jit(solution)/shard_map/ppermute | solution.py:135
  96.6 39.6 %collective-permute-start.2 = (bf16[256,512]{1,0:T(8,128)(2,1)S(1)}, bf16[256,512]{1,0:T(8,128)(2,1)}, u32[]{:S(2)}, u32[]{:S(2)}) collective-permute-start(bf16[256,512]{1,0:T(8,128)(2,1)S(1)} %get-tuple-element.76), channel_id=1, source_target_pairs={{0,4},{4,0},{8,12},{12,8},{16,20},{20,16},{24,28},{28,24},{1,5},{5... | collective-permute-start | bytes 786440 | tf_op jit(solution)/shard_map/ppermute | solution.py:135
  105.5 30.7 %collective-permute-start.3 = (bf16[256,512]{1,0:T(8,128)(2,1)}, bf16[256,512]{1,0:T(8,128)(2,1)}, u32[]{:S(2)}, u32[]{:S(2)}) collective-permute-start(bf16[256,512]{1,0:T(8,128)(2,1)} %collective-permute-done.1), channel_id=1, source_target_pairs={{0,4},{4,0},{8,12},{12,8},{16,20},{20,16},{24,28},{28,24},{1,5},{5... | collective-permute-start | bytes 786440 | tf_op jit(solution)/shard_map/ppermute | solution.py:135
  227.3 228.9 %collective-permute-start.77 = (bf16[2,2,256,512]{3,2,0,1:T(8,128)(2,1)}, bf16[2,2,256,512]{3,2,0,1:T(8,128)(2,1)}, u32[]{:S(2)}, u32[]{:S(2)}) collective-permute-start(bf16[2,2,256,512]{3,2,0,1:T(8,128)(2,1)} %bitcast.450), channel_id=1, source_target_pairs={{0,4},{4,0},{8,12},{12,8},{16,20},{20,16},{24,28},{28,24},{1,5},{5... | collective-permute-start | bytes 3145736 | tf_op jit(solution)/shard_map/ppermute | solution.py:135
  229.3 224.2 %collective-permute-start.72 = (bf16[2,2,64,2048]{3,2,1,0:T(8,128)(2,1)}, bf16[2,2,64,2048]{3,2,1,0:T(8,128)(2,1)}, u32[]{:S(2)}, u32[]{:S(2)}) collective-permute-start(bf16[2,2,64,2048]{3,2,1,0:T(8,128)(2,1)} %dynamic-slice_bitcast_fusion), channel_id=1, source_target_pairs={{0,4},{4,0},{8,12},{12,8},{16,20},{20,16},{24,28},{28,24},{1,5},{5... | collective-permute-start | bytes 3145736 | tf_op jit(solution)/shard_map/ppermute | solution.py:135
  230.4 55.2 %collective-permute-start.67 = (bf16[2,2,64,512]{3,2,0,1:T(8,128)(2,1)}, bf16[2,2,64,512]{3,2,0,1:T(8,128)(2,1)}, u32[]{:S(2)}, u32[]{:S(2)}) collective-permute-start(bf16[2,2,64,512]{3,2,0,1:T(8,128)(2,1)} %bitcast.452), channel_id=1, source_target_pairs={{0,4},{4,0},{8,12},{12,8},{16,20},{20,16},{24,28},{28,24},{1,5},{5... | collective-permute-start | bytes 786440 | tf_op jit(solution)/shard_map/ppermute | solution.py:135
  231.4 113.0 %collective-permute-start.62 = (bf16[2,2,64,1024]{3,2,1,0:T(8,128)(2,1)}, bf16[2,2,64,1024]{3,2,1,0:T(8,128)(2,1)}, u32[]{:S(2)}, u32[]{:S(2)}) collective-permute-start(bf16[2,2,64,1024]{3,2,1,0:T(8,128)(2,1)} %dynamic-slice_bitcast_fusion.4), channel_id=1, source_target_pairs={{0,4},{4,0},{8,12},{12,8},{16,20},{20,16},{24,28},{28,24},{1,5},{5... | collective-permute-start | bytes 1572872 | tf_op jit(solution)/shard_map/ppermute | solution.py:135
  286.7 55.4 %collective-permute-start.14 = (bf16[2,256,512]{2,1,0:T(8,128)(2,1)S(1)}, bf16[2,256,512]{2,1,0:T(8,128)(2,1)S(1)}, u32[]{:S(2)}, u32[]{:S(2)}) collective-permute-start(bf16[2,256,512]{2,1,0:T(8,128)(2,1)S(1)} %pad_maximum_fusion.15), channel_id=1, source_target_pairs={{0,4},{4,0},{8,12},{12,8},{16,20},{20,16},{24,28},{28,24},{1,5},{5... | collective-permute-start | bytes 1572872 | tf_op jit(solution)/shard_map/ppermute | solution.py:135
  346.5 34.7 %collective-permute-start.63 = (bf16[2,64,1024]{2,1,0:T(8,128)(2,1)}, bf16[2,64,1024]{2,1,0:T(8,128)(2,1)}, u32[]{:S(2)}, u32[]{:S(2)}) collective-permute-start(bf16[2,64,1024]{2,1,0:T(8,128)(2,1)} %dynamic-slice_bitcast_fusion.11), channel_id=1, source_target_pairs={{0,16},{4,20},{8,24},{12,28},{16,0},{20,4},{24,8},{28,12},{1,17},{... | collective-permute-start | bytes 786440 | tf_op jit(solution)/shard_map/ppermute | solution.py:135
  350.4 36.1 %collective-permute-start.20 = (bf16[256,512]{1,0:T(8,128)(2,1)}, bf16[256,512]{1,0:T(8,128)(2,1)}, u32[]{:S(2)}, u32[]{:S(2)}) collective-permute-start(bf16[256,512]{1,0:T(8,128)(2,1)} %fusion.145), channel_id=1, source_target_pairs={{0,1},{1,0},{2,3},{3,2},{4,5},{5,4},{6,7},{7,6},{8,9},{9,8},{10,11... | collective-permute-start | bytes 786440 | tf_op jit(solution)/shard_map/ppermute | solution.py:135
  383.9 55.0 %collective-permute-start.64 = (bf16[64,1024]{1,0:T(8,128)(2,1)}, bf16[64,1024]{1,0:T(8,128)(2,1)S(1)}, u32[]{:S(2)}, u32[]{:S(2)}) collective-permute-start(bf16[64,1024]{1,0:T(8,128)(2,1)} %dynamic-slice_bitcast_fusion.29), channel_id=1, source_target_pairs={{0,8},{4,12},{8,0},{12,4},{16,24},{20,28},{24,16},{28,20},{1,9},{5... | collective-permute-start | bytes 393224 | tf_op jit(solution)/shard_map/ppermute | solution.py:135
  394.6 106.4 %collective-permute-start.47 = (bf16[2,2,64,1536]{3,2,1,0:T(8,128)(2,1)}, bf16[2,2,64,1536]{3,2,1,0:T(8,128)(2,1)}, u32[]{:S(2)}, u32[]{:S(2)}) collective-permute-start(bf16[2,2,64,1536]{3,2,1,0:T(8,128)(2,1)} %fusion.74), channel_id=1, source_target_pairs={{0,4},{4,0},{8,12},{12,8},{16,20},{20,16},{24,28},{28,24},{1,5},{5... | collective-permute-start | bytes 2359304 | tf_op jit(solution)/shard_map/ppermute | solution.py:135
  396.5 55.3 %collective-permute-start.32 = (bf16[2,2,64,512]{3,2,0,1:T(8,128)(2,1)}, bf16[2,2,64,512]{3,2,0,1:T(8,128)(2,1)}, u32[]{:S(2)}, u32[]{:S(2)}) collective-permute-start(bf16[2,2,64,512]{3,2,0,1:T(8,128)(2,1)} %bitcast.455), channel_id=1, source_target_pairs={{0,4},{4,0},{8,12},{12,8},{16,20},{20,16},{24,28},{28,24},{1,5},{5... | collective-permute-start | bytes 786440 | tf_op jit(solution)/shard_map/ppermute | solution.py:135
  450.5 82.7 %collective-permute-start.42 = (bf16[2,2,256,512]{3,2,0,1:T(8,128)(2,1)}, bf16[2,2,256,512]{3,2,0,1:T(8,128)(2,1)}, u32[]{:S(2)}, u32[]{:S(2)}) collective-permute-start(bf16[2,2,256,512]{3,2,0,1:T(8,128)(2,1)} %bitcast.521), channel_id=1, source_target_pairs={{0,4},{4,0},{8,12},{12,8},{16,20},{20,16},{24,28},{28,24},{1,5},{5... | collective-permute-start | bytes 3145736 | tf_op jit(solution)/shard_map/ppermute | solution.py:135
  451.9 24.5 %collective-permute-start.16 = (bf16[2,256,512]{2,1,0:T(8,128)(2,1)}, bf16[2,256,512]{2,1,0:T(8,128)(2,1)S(1)}, u32[]{:S(2)}, u32[]{:S(2)}) collective-permute-start(bf16[2,256,512]{2,1,0:T(8,128)(2,1)} %pad_maximum_fusion.16), channel_id=1, source_target_pairs={{0,4},{4,0},{8,12},{12,8},{16,20},{20,16},{24,28},{28,24},{1,5},{5... | collective-permute-start | bytes 1572872 | tf_op jit(solution)/shard_map/ppermute | solution.py:135
  465.6 14.3 %collective-permute-start.78 = (bf16[2,256,512]{2,1,0:T(8,128)(2,1)S(1)}, bf16[2,256,512]{2,1,0:T(8,128)(2,1)S(1)}, u32[]{:S(2)}, u32[]{:S(2)}) collective-permute-start(bf16[2,256,512]{2,1,0:T(8,128)(2,1)S(1)} %dynamic-slice_bitcast_fusion.2), channel_id=1, source_target_pairs={{0,8},{4,12},{8,0},{12,4},{16,24},{20,28},{24,16},{28,20},{1,9},{5... | collective-permute-start | bytes 1572872 | tf_op jit(solution)/shard_map/ppermute | solution.py:135
  475.7 51.4 %collective-permute-start.37 = (bf16[2,2,64,2048]{3,2,1,0:T(8,128)(2,1)}, bf16[2,2,64,2048]{3,2,1,0:T(8,128)(2,1)}, u32[]{:S(2)}, u32[]{:S(2)}) collective-permute-start(bf16[2,2,64,2048]{3,2,1,0:T(8,128)(2,1)} %dynamic-slice_bitcast_fusion.1), channel_id=1, source_target_pairs={{0,4},{4,0},{8,12},{12,8},{16,20},{20,16},{24,28},{28,24},{1,5},{5... | collective-permute-start | bytes 3145736 | tf_op jit(solution)/shard_map/ppermute | solution.py:135
  476.3 14.3 %collective-permute-start.73 = (bf16[2,64,2048]{2,1,0:T(8,128)(2,1)S(1)}, bf16[2,64,2048]{2,1,0:T(8,128)(2,1)S(1)}, u32[]{:S(2)}, u32[]{:S(2)}) collective-permute-start(bf16[2,64,2048]{2,1,0:T(8,128)(2,1)S(1)} %dynamic-slice_bitcast_fusion.3), channel_id=1, source_target_pairs={{0,16},{4,20},{8,24},{12,28},{16,0},{20,4},{24,8},{28,12},{1,17},{... | collective-permute-start | bytes 1572872 | tf_op jit(solution)/shard_map/ppermute | solution.py:135
  490.7 33.4 %collective-permute-start.79 = (bf16[256,512]{1,0:T(8,128)(2,1)}, bf16[256,512]{1,0:T(8,128)(2,1)}, u32[]{:S(2)}, u32[]{:S(2)}) collective-permute-start(bf16[256,512]{1,0:T(8,128)(2,1)} %dynamic-slice_bitcast_fusion.9), channel_id=1, source_target_pairs={{0,16},{4,20},{8,24},{12,28},{16,0},{20,4},{24,8},{28,12},{1,17},{... | collective-permute-start | bytes 786440 | tf_op jit(solution)/shard_map/ppermute | solution.py:135
  493.2 32.0 %collective-permute-start.74 = (bf16[64,2048]{1,0:T(8,128)(2,1)}, bf16[64,2048]{1,0:T(8,128)(2,1)}, u32[]{:S(2)}, u32[]{:S(2)}) collective-permute-start(bf16[64,2048]{1,0:T(8,128)(2,1)} %dynamic-slice_bitcast_fusion.10), channel_id=1, source_target_pairs={{0,8},{4,12},{8,0},{12,4},{16,24},{20,28},{24,16},{28,20},{1,9},{5... | collective-permute-start | bytes 786440 | tf_op jit(solution)/shard_map/ppermute | solution.py:135
  519.4 29.7 %collective-permute-start.48 = (bf16[2,64,1536]{2,1,0:T(8,128)(2,1)}, bf16[2,64,1536]{2,1,0:T(8,128)(2,1)}, u32[]{:S(2)}, u32[]{:S(2)}) collective-permute-start(bf16[2,64,1536]{2,1,0:T(8,128)(2,1)} %dynamic-slice_bitcast_fusion.7), channel_id=1, source_target_pairs={{0,16},{4,20},{8,24},{12,28},{16,0},{20,4},{24,8},{28,12},{1,17},{... | collective-permute-start | bytes 1179656 | tf_op jit(solution)/shard_map/ppermute | solution.py:135
  524.0 50.2 %collective-permute-start.27 = (bf16[2,2,64,1536]{3,2,1,0:T(8,128)(2,1)}, bf16[2,2,64,1536]{3,2,1,0:T(8,128)(2,1)S(1)}, u32[]{:S(2)}, u32[]{:S(2)}) collective-permute-start(bf16[2,2,64,1536]{3,2,1,0:T(8,128)(2,1)} %fusion.78), channel_id=1, source_target_pairs={{0,4},{4,0},{8,12},{12,8},{16,20},{20,16},{24,28},{28,24},{1,5},{5... | collective-permute-start | bytes 2359304 | tf_op jit(solution)/shard_map/ppermute | solution.py:135
  527.2 20.3 %collective-permute-start.80 = (bf16[256,256]{1,0:T(8,128)(2,1)S(1)}, bf16[256,256]{1,0:T(8,128)(2,1)S(1)}, u32[]{:S(2)}, u32[]{:S(2)}) collective-permute-start(bf16[256,256]{1,0:T(8,128)(2,1)S(1)} %dynamic-slice_convert_fusion.6), channel_id=1, source_target_pairs={{0,2},{1,3},{2,0},{3,1},{4,6},{5,7},{6,4},{7,5},{8,10},{9,11},{10,... | collective-permute-start | bytes 393224 | tf_op jit(solution)/shard_map/ppermute | solution.py:135
  533.1 17.2 %collective-permute-start.75 = (bf16[64,1024]{1,0:T(8,128)(2,1)S(1)}, bf16[64,1024]{1,0:T(8,128)(2,1)S(1)}, u32[]{:S(2)}, u32[]{:S(2)}) collective-permute-start(bf16[64,1024]{1,0:T(8,128)(2,1)S(1)} %dynamic-slice_convert_fusion.7), channel_id=1, source_target_pairs={{0,2},{1,3},{2,0},{3,1},{4,6},{5,7},{6,4},{7,5},{8,10},{9,11},{10,... | collective-permute-start | bytes 393224 | tf_op jit(solution)/shard_map/ppermute | solution.py:135
  534.9 36.9 %collective-permute-start.43 = (bf16[2,256,512]{2,1,0:T(8,128)(2,1)S(1)}, bf16[2,256,512]{2,1,0:T(8,128)(2,1)S(1)}, u32[]{:S(2)}, u32[]{:S(2)}) collective-permute-start(bf16[2,256,512]{2,1,0:T(8,128)(2,1)S(1)} %dynamic-slice_bitcast_fusion.5), channel_id=1, source_target_pairs={{0,8},{4,12},{8,0},{12,4},{16,24},{20,28},{24,16},{28,20},{1,9},{5... | collective-permute-start | bytes 1572872 | tf_op jit(solution)/shard_map/ppermute | solution.py:135
  547.5 26.0 %collective-permute-start.38 = (bf16[2,64,2048]{2,1,0:T(8,128)(2,1)S(1)}, bf16[2,64,2048]{2,1,0:T(8,128)(2,1)S(1)}, u32[]{:S(2)}, u32[]{:S(2)}) collective-permute-start(bf16[2,64,2048]{2,1,0:T(8,128)(2,1)S(1)} %dynamic-slice_bitcast_fusion.6), channel_id=1, source_target_pairs={{0,16},{4,20},{8,24},{12,28},{16,0},{20,4},{24,8},{28,12},{1,17},{... | collective-permute-start | bytes 1572872 | tf_op jit(solution)/shard_map/ppermute | solution.py:135
  574.6 14.7 %collective-permute-start.28 = (bf16[2,64,1536]{2,1,0:T(8,128)(2,1)S(1)}, bf16[2,64,1536]{2,1,0:T(8,128)(2,1)S(1)}, u32[]{:S(2)}, u32[]{:S(2)}) collective-permute-start(bf16[2,64,1536]{2,1,0:T(8,128)(2,1)S(1)} %dynamic-slice_bitcast_fusion.8), channel_id=1, source_target_pairs={{0,16},{4,20},{8,24},{12,28},{16,0},{20,4},{24,8},{28,12},{1,17},{... | collective-permute-start | bytes 1179656 | tf_op jit(solution)/shard_map/ppermute | solution.py:135
  (209 other events, 1559.4 us)
